TPU v7x, 512 devices: a whole 4x4x16 slice. The times are simulated.
512 devices in a mesh: region: 8 (over z_hi, x), blk: 64 (over y, z_lo, core).
Axes of the slice: x: 4, y: 4, z: 16 (z_hi: 2, z_lo: 8; z = z_hi * 8 + z_lo), core: 2. Of those that a mesh axis runs over, the one named last changes fastest.
Arguments:
- records: float32 [2048, 2048], P(('region', 'blk')), may hold values from -6 to 6
- starts: int32 [2048], P(('region', 'blk')), may hold values from 0 to 1024
- tapers: int32 [2048], P(('region', 'blk')), may hold values from 2 to 256
- pair_a: int32 [393216], P(('region', 'blk')), may hold values from 0 to 3
- pair_b: int32 [393216], P(('region', 'blk')), may hold values from 0 to 255
- pair_count: int32 [512], P(('region', 'blk')), may hold values from 192 to 768, as said below
- observed: float32 [393216, 512], P(('region', 'blk')), may hold values from -6 to 6
Outputs:
- correlations: float32 [393216, 512], P(('region', 'blk'))
- far_correlations: float32 [2048, 512], P(('region', 'blk'))
- adjoint: float32 [2048, 1024], P(('region', 'blk'))
Inputs may be any that keep to these rules, and one draw needn't show every extreme that they name: `pair_count`: device 0 has all 768 slots live.
All inputs are finite; a program needn't handle non-finite values.
Results may differ from a plain program's by a relative error of at most 0.0003.
Values sent between devices are 32-bit elements; how exact they have to be, the bound alone decides.
A program may use at most 64 MiB of HBM per device.

v0:
```python
import math
import jax
import jax.numpy as jnp
from jax import lax
from jax.sharding import PartitionSpec as P

WIN = 1024


def shifted(shard, axis, by):
    size = lax.axis_size(axis)
    return lax.ppermute(shard, axis, [(i, (i + by) % size) for i in range(size)])


def phase_table(rows, cols, length):
    product = rows[:, None] * cols[None, :] % length
    return product.astype(jnp.float32) * (2.0 * math.pi / length)


def taper_windows(records, starts, tapers):
    sample = jnp.arange(WIN, dtype=jnp.int32)
    picked = jnp.take_along_axis(records, starts[:, None] + sample[None, :], axis=1)
    lengths = tapers.astype(jnp.float32)[:, None]
    position = sample.astype(jnp.float32)[None, :]
    shape_fn = jnp.minimum(1.0, jnp.minimum((position + 1.0) / lengths, (WIN - position) / lengths))
    return picked * shape_fn * WIN ** (-0.25)


def to_spectra(windows):
    angle = phase_table(
        jnp.arange(WIN, dtype=jnp.int32), jnp.arange(WIN // 2, dtype=jnp.int32), WIN
    )
    real_part = jnp.dot(windows, jnp.cos(angle), precision=lax.Precision.HIGHEST)
    imag_part = jnp.dot(windows, -jnp.sin(angle), precision=lax.Precision.HIGHEST)
    return jnp.concatenate([real_part, imag_part], axis=1)


def bin_weights():
    bins = jnp.arange(WIN // 2, dtype=jnp.int32)
    weight = jnp.where(bins == 0, 1.0, 2.0).astype(jnp.float32) / WIN
    return jnp.concatenate([weight, weight])


def lag_index():
    return (jnp.arange(WIN // 2, dtype=jnp.int32) - WIN // 4) % WIN


def to_lags(cross_spec):
    angle = phase_table(jnp.arange(WIN // 2, dtype=jnp.int32), lag_index(), WIN)
    table = jnp.concatenate([jnp.cos(angle), -jnp.sin(angle)], axis=0)
    return jnp.dot(cross_spec * bin_weights()[None, :], table, precision=lax.Precision.HIGHEST)


def from_lags(residual):
    angle = phase_table(lag_index(), jnp.arange(WIN // 2, dtype=jnp.int32), WIN)
    table = jnp.concatenate([jnp.cos(angle), -jnp.sin(angle)], axis=1)
    return jnp.dot(residual, table, precision=lax.Precision.HIGHEST)


def to_time(source):
    half = WIN // 2
    angle = phase_table(jnp.arange(half, dtype=jnp.int32), jnp.arange(WIN, dtype=jnp.int32), WIN)
    weighted = source * bin_weights()[None, :]
    first = jnp.dot(weighted[:, :half], jnp.cos(angle), precision=lax.Precision.HIGHEST)
    second = jnp.dot(weighted[:, half:], jnp.sin(angle), precision=lax.Precision.HIGHEST)
    return (first - second) * (1.0 / 16.0)


def cross(left, right):
    half = WIN // 2
    left_r, left_i = (left[:, :half], left[:, half:])
    right_r, right_i = (right[:, :half], right[:, half:])
    return jnp.concatenate(
        [left_r * right_r + left_i * right_i, left_i * right_r - left_r * right_i], axis=1
    )


def times_plain(misfit, spec):
    half = WIN // 2
    mis_r, mis_i = (misfit[:, :half], misfit[:, half:])
    spec_r, spec_i = (spec[:, :half], spec[:, half:])
    return jnp.concatenate(
        [mis_r * spec_r - mis_i * spec_i, mis_r * spec_i + mis_i * spec_r], axis=1
    )


def times_conj(misfit, spec):
    half = WIN // 2
    mis_r, mis_i = (misfit[:, :half], misfit[:, half:])
    spec_r, spec_i = (spec[:, :half], spec[:, half:])
    return jnp.concatenate(
        [mis_r * spec_r + mis_i * spec_i, mis_r * spec_i - mis_i * spec_r], axis=1
    )


def body(records, starts, tapers, pair_a, pair_b, pair_count, observed):
    stations = records.shape[0]
    blocks = lax.axis_size("blk")
    slots = pair_a.shape[0]
    windows = taper_windows(records, starts, tapers)
    spectra = to_spectra(windows)
    group_spec = lax.all_gather(spectra, "blk", axis=0, tiled=True)
    prior = shifted(spectra, "region", 1)
    source_spec = jnp.take(spectra, pair_a, axis=0)
    target_spec = jnp.take(group_spec, pair_b, axis=0)
    live_rows = (jnp.arange(slots, dtype=jnp.int32) < pair_count[0]).astype(jnp.float32)[:, None]
    corr_raw = to_lags(cross(source_spec, target_spec))
    misfit = from_lags((corr_raw - observed) * live_rows)
    group_onehot = (
        jnp.arange(stations * blocks, dtype=jnp.int32)[:, None] == pair_b[None, :]
    ).astype(jnp.float32)
    remote_terms = jnp.dot(
        group_onehot, times_conj(misfit, source_spec), precision=lax.Precision.HIGHEST
    )
    own_onehot = (jnp.arange(stations, dtype=jnp.int32)[:, None] == pair_a[None, :]).astype(
        jnp.float32
    )
    local_terms = jnp.dot(
        own_onehot, times_plain(misfit, target_spec), precision=lax.Precision.HIGHEST
    )
    far_correlations = to_lags(cross(spectra, prior))
    returned = lax.psum_scatter(remote_terms, "blk", scatter_dimension=0, tiled=True)
    adjoint = to_time(local_terms + returned)
    return (corr_raw * live_rows, far_correlations, adjoint)


def solution(mesh):
    in_specs = (
        P(("region", "blk"), None),
        P(("region", "blk")),
        P(("region", "blk")),
        P(("region", "blk")),
        P(("region", "blk")),
        P(("region", "blk")),
        P(("region", "blk"), None),
    )
    out_specs = (P(("region", "blk"), None), P(("region", "blk"), None), P(("region", "blk"), None))
    return jax.shard_map(body, mesh=mesh, in_specs=in_specs, out_specs=out_specs, check_vma=False)
```

profile of v0, /device:TPU:1, one launch (start us, length us, event | category | flops | bytes accessed | tf_op | source)
XLA Modules:
  0.0 1073.0 jit_solution(7538603702445230818)
XLA Ops:
  7.2 0.0 copy-start
  7.2 0.0 all-gather.3.cloned.1.call-start
  7.2 0.7 fusion.78
  8.0 0.0 copy-done
  8.0 0.0 copy-start.10
  8.0 0.0 copy-start.9
  8.0 34.9 %gather_fusion.2 = f32[4096]{0:T(1024)S(1)} fusion(f32[4,2048]{1,0:T(4,128)S(1)} %copy-done, s32[4096]{0:T(1024)S(1)} %bitcast.13), kind=kCustom, calls=%fused_computation.2 | custom fusion | bytes 65536 | tf_op jit(solution)/shard_map/jit(take_along_axis)/gather | solution.py:22
  43.0 0.0 copy-done.10
  43.0 0.0 copy-done.9
  43.0 0.1 fusion.74
  43.1 8.9 fusion.27
  51.9 0.0 copy-start.8
  52.0 8.7 fusion.30
  60.7 0.6 pad_maximum_fusion.3
  61.3 0.0 all-gather.3.cloned.1.call-update
  61.3 0.2 all-reduce.3.cloned.1.call-start
  62.2 0.0 copy-done.8
  62.2 0.0 copy-start.7
  62.2 2.5 gather_fusion
  64.8 0.0 copy-done.7
  64.9 9.3 fusion.69
  74.2 1.9 broadcast_select_fusion.1
  76.1 111.2 %all-gather.3.cloned.1.call-done = f32[64,4,1024]{2,1,0:T(4,128)} async-done(((f32[1,4,1024]{2,1,0:T(4,128)}), f32[64,4,1024]{2,1,0:T(4,128)}) %all-gather.3.cloned.1.call-update) | async-done | bytes 1048592 | tf_op jit(solution)/shard_map/all_gather | solution.py:102
  187.3 1.6 reshape.148
  188.9 3.6 gather_fusion.1
  192.5 0.0 copy-start.1
  192.5 2.3 broadcast_select_fusion
  194.9 0.5 copy-done.1
  195.4 0.0 copy-start.2
  195.4 0.0 copy-start.3
  195.4 0.8 multiply_add_fusion.2
  196.2 0.4 copy-done.2
  196.6 0.3 copy-done.3
  196.9 0.0 copy-start.4
  196.9 0.0 copy-start.5
  196.9 0.0 copy-start.6
  196.9 6.2 broadcast_multiply_fusion
  203.2 0.0 copy-done.4
  203.2 0.0 copy-done.5
  203.2 0.0 copy-done.6
  203.2 5.3 fusion.17
  208.4 3.1 multiply_add_fusion
  211.5 3.0 fusion.7
  214.6 0.0 all-reduce.3.cloned.1.call-update
  214.6 3.1 collective-permute-start
  217.7 1.3 dynamic-slice
  219.6 10.3 collective-permute-done
  230.0 1.7 fusion.36
  231.7 812.9 %all-reduce.3.cloned.1.call-done = f32[256,1024]{1,0:T(8,128)} async-done(((f32[256,1024]{1,0:T(8,128)}), f32[256,1024]{1,0:T(8,128)}) %all-reduce.3.cloned.1.call-update) | async-done | bytes 1048592
  1044.5 3.0 fusion.49
  1047.5 9.0 fusion.21
  1056.5 9.7 fusion.43
  (15 shorter events, 0.1 us)
Async XLA Ops:
  7.2 0.8 copy-start
  7.2 180.1 %all-gather.3.cloned.1.call-start = ((), (), s32[]{:S(2)}) async-start(), calls=%async_computation | async-start | bytes 1064960 | tf_op jit(solution)/shard_map/all_gather | solution.py:102
  8.0 35.0 %copy-start.10 = (s32[4]{0:T(128)S(1)}, s32[4]{0:T(128)}, u32[]{:S(2)}) copy-start(s32[4]{0:T(128)} %param.9) | copy-start | bytes 52
  8.0 35.0 %copy-start.9 = (s32[4]{0:T(128)S(1)}, s32[4]{0:T(128)}, u32[]{:S(2)}) copy-start(s32[4]{0:T(128)} %param.8) | copy-start | bytes 52
  51.9 10.2 copy-start.8
  61.3 983.2 %all-reduce.3.cloned.1.call-start = ((), (), s32[]{:S(2)}) async-start(), calls=%async_computation.1 | async-start | bytes 2097152
  62.2 2.6 copy-start.7
  192.5 2.8 copy-start.1
  195.4 1.2 copy-start.2
  195.4 1.5 copy-start.3
  196.9 6.3 copy-start.4
  196.9 6.3 copy-start.5
  196.9 6.3 copy-start.6
  214.6 15.4 %collective-permute-start = (f32[4,1024]{1,0:T(4,128)S(1)}, f32[4,1024]{1,0:T(4,128)S(1)}, u32[]{:S(2)}, u32[]{:S(2)}) collective-permute-start(f32[4,1024]{1,0:T(4,128)S(1)} %get-tuple-element.13), channel_id=1, source_target_pairs={{0,64},{64,128},{128,192},{192,256},{256,320},{320,384},{384,448},... | collective-permute-start | bytes 49160 | tf_op jit(solution)/shard_map/ppermute | solution.py:12
Sparse Core Ops, SparseCore 0:
  61.4 125.8 all-gather.2
  214.7 829.7 all-reduce.2
where the time goes:
time: 1070 us
  waiting for transfers between devices  934 us (87%)
  matrix products  55.5 us (5%)
  local copies, waits for them, and re-layouts  45.2 us (4%)
  other arithmetic  19 us (2%)
  between operations  15.6 us (1%)
    unnamed x3, waiting for transfers between devices  813 us
    all_gather x1, waiting for transfers between devices, body(): group_spec = lax.all_gather(spectra, 'blk', axis=0, tiled=True)  111 us
    gather x2, local copies, waits for them, and re-layouts, taper_windows(): jnp.take_along_axis(records, starts[:, None] + sample[None, :], axis=1)  34.9 us
  transfers between devices with their start and end apart: 3, of which 3 were waited for; matrix products, arithmetic and copies ran while one was open for 2% of the time, Pallas kernels for 0%

commit v1 on v0

--- a/solution.py
+++ b/solution.py
@@ -99,7 +99,9 @@
     slots = pair_a.shape[0]
     windows = taper_windows(records, starts, tapers)
     spectra = to_spectra(windows)
-    group_spec = lax.all_gather(spectra, "blk", axis=0, tiled=True)
+    w1 = jnp.stack([spectra for _ in range(lax.axis_size("blk"))])
+    extra = lax.all_to_all(w1, "blk", 0, 0)
+    group_spec = jnp.concatenate(extra, axis=0)
     prior = shifted(spectra, "region", 1)
     source_spec = jnp.take(spectra, pair_a, axis=0)
     target_spec = jnp.take(group_spec, pair_b, axis=0)

time: 1070 us -> 1020 us (0.953)
  waiting for transfers between devices: 934 us -> 860 us
  starting transfers between devices: 3.36 us -> 20.7 us
    all_gather x1 -> x0, waiting for transfers between devices: 111 us -> none  [body(): group_spec = lax.all_gather(spectra, 'blk', axis=0, tiled=True)]
    all_to_all x0 -> x1, waiting for transfers between devices: none -> 36.4 us  [body(): extra = lax.all_to_all(w1, 'blk', 0, 0)]
    all_to_all x0 -> x1, starting transfers between devices: none -> 17.4 us  [body(): extra = lax.all_to_all(w1, 'blk', 0, 0)]
    unnamed x3 -> x2, waiting for transfers between devices: 813 us -> 814 us
where the time goes in v1:
time: 1020 us
  waiting for transfers between devices  860 us (84%)
  matrix products  55.5 us (5%)
  local copies, waits for them, and re-layouts  46.5 us (5%)
  starting transfers between devices  20.7 us (2%)
  other arithmetic  18.4 us (2%)
  between operations  15.6 us (2%)
    unnamed x2, waiting for transfers between devices  814 us
    all_to_all x1, waiting for transfers between devices, body(): extra = lax.all_to_all(w1, 'blk', 0, 0)  36.4 us
    gather x2, local copies, waits for them, and re-layouts, taper_windows(): jnp.take_along_axis(records, starts[:, None] + sample[None, :], axis=1)  34.9 us
  transfers between devices with their start and end apart: 3, of which 3 were waited for; matrix products, arithmetic and copies ran while one was open for 2% of the time, Pallas kernels for 0%

profile of v1, /device:TPU:1, one launch (start us, length us, event | category | flops | bytes accessed | tf_op | source)
XLA Modules:
  0.0 1017.1 jit_solution(12237314966877421504)
XLA Ops:
  7.2 0.0 copy-start
  7.2 0.7 fusion.78
  7.9 0.0 copy-done
  8.0 0.0 copy-start.10
  8.0 0.0 copy-start.9
  8.0 34.9 %gather_fusion.2 = f32[4096]{0:T(1024)S(1)} fusion(f32[4,2048]{1,0:T(4,128)S(1)} %copy-done, s32[4096]{0:T(1024)S(1)} %bitcast.11), kind=kCustom, calls=%fused_computation.2 | custom fusion | bytes 65536 | tf_op jit(solution)/shard_map/jit(take_along_axis)/gather | solution.py:22
  42.9 0.0 copy-done.10
  42.9 0.0 copy-done.9
  43.0 0.1 fusion.74
  43.1 8.9 fusion.27
  51.9 8.7 fusion.30
  60.6 0.0 copy-start.8
  60.6 1.2 stack.2
  61.9 17.4 %all-to-all-start = ((f32[64,4,1024]{2,1,0:T(4,128)}), f32[64,4,1024]{2,1,0:T(4,128)}, u32[]{:S(2)}, u32[]{:S(2)}) async-start(f32[64,4,1024]{2,1,0:T(4,128)} %stack.2), calls=%async_computation | async-start | bytes 2097152 | tf_op jit(solution)/shard_map/all_to_all | solution.py:103
  79.3 0.2 all-reduce.3.cloned.1.call-start
  80.2 0.0 copy-done.8
  80.2 0.0 copy-start.7
  80.2 2.5 gather_fusion
  82.7 0.0 copy-done.7
  82.8 9.3 fusion.69
  92.2 1.9 broadcast_select_fusion.1
  94.1 36.4 %all-to-all-done = f32[64,4,1024]{2,1,0:T(4,128)} async-done(((f32[64,4,1024]{2,1,0:T(4,128)}), f32[64,4,1024]{2,1,0:T(4,128)}, u32[]{:S(2)}, u32[]{:S(2)}) %all-to-all-start) | async-done | bytes 1048608 | tf_op jit(solution)/shard_map/all_to_all | solution.py:103
  130.5 1.6 reshape.128
  132.1 3.7 gather_fusion.1
  135.7 0.0 copy-start.1
  135.7 2.3 broadcast_select_fusion
  138.1 0.5 copy-done.1
  138.6 0.0 copy-start.2
  138.6 0.0 copy-start.3
  138.6 0.8 multiply_add_fusion.2
  139.4 0.4 copy-done.2
  139.8 0.3 copy-done.3
  140.1 0.0 copy-start.4
  140.1 0.0 copy-start.5
  140.1 0.0 copy-start.6
  140.1 6.2 broadcast_multiply_fusion
  146.4 0.0 copy-done.4
  146.4 0.0 copy-done.5
  146.4 0.0 copy-done.6
  146.4 5.3 fusion.17
  151.6 3.1 multiply_add_fusion
  154.8 3.0 fusion.7
  157.8 0.0 all-reduce.3.cloned.1.call-update
  157.8 3.1 collective-permute-start
  160.9 1.3 dynamic-slice
  162.8 10.3 %collective-permute-done = f32[4,1024]{1,0:T(4,128)S(1)} collective-permute-done((f32[4,1024]{1,0:T(4,128)S(1)}, f32[4,1024]{1,0:T(4,128)S(1)}, u32[]{:S(2)}, u32[]{:S(2)}) %collective-permute-start) | collective-permute-done | bytes 16416 | tf_op jit(solution)/shard_map/ppermute | solution.py:12
  173.1 1.7 fusion.36
  174.8 813.8 %all-reduce.3.cloned.1.call-done = f32[256,1024]{1,0:T(8,128)} async-done(((f32[256,1024]{1,0:T(8,128)}), f32[256,1024]{1,0:T(8,128)}) %all-reduce.3.cloned.1.call-update) | async-done | bytes 1048592
  988.6 3.0 fusion.49
  991.6 9.0 fusion.21
  1000.6 9.7 fusion.43
  (16 shorter events, 0.1 us)
Async XLA Ops:
  7.2 0.8 copy-start
  8.0 35.0 %copy-start.10 = (s32[4]{0:T(128)S(1)}, s32[4]{0:T(128)}, u32[]{:S(2)}) copy-start(s32[4]{0:T(128)} %param.9) | copy-start | bytes 52
  8.0 35.0 %copy-start.9 = (s32[4]{0:T(128)S(1)}, s32[4]{0:T(128)}, u32[]{:S(2)}) copy-start(s32[4]{0:T(128)} %param.8) | copy-start | bytes 52
  60.6 19.5 %copy-start.8 = (s32[768]{0:T(1024)S(1)}, s32[768]{0:T(1024)}, u32[]{:S(2)}) copy-start(s32[768]{0:T(1024)} %param.10) | copy-start | bytes 9220
  61.9 68.6 %all-to-all-start = ((f32[64,4,1024]{2,1,0:T(4,128)}), f32[64,4,1024]{2,1,0:T(4,128)}, u32[]{:S(2)}, u32[]{:S(2)}) async-start(f32[64,4,1024]{2,1,0:T(4,128)} %stack.2), calls=%async_computation | async-start | bytes 2097152 | tf_op jit(solution)/shard_map/all_to_all | solution.py:103
  79.3 909.3 %all-reduce.3.cloned.1.call-start = ((), (), s32[]{:S(2)}) async-start(), calls=%async_computation.1 | async-start | bytes 2097152
  80.2 2.6 copy-start.7
  135.7 2.8 copy-start.1
  138.6 1.2 copy-start.2
  138.6 1.5 copy-start.3
  140.1 6.3 copy-start.4
  140.1 6.3 copy-start.5
  140.1 6.3 copy-start.6
  157.8 15.3 %collective-permute-start = (f32[4,1024]{1,0:T(4,128)S(1)}, f32[4,1024]{1,0:T(4,128)S(1)}, u32[]{:S(2)}, u32[]{:S(2)}) collective-permute-start(f32[4,1024]{1,0:T(4,128)S(1)} %pad_maximum_fusion.3), channel_id=1, source_target_pairs={{0,64},{64,128},{128,192},{192,256},{256,320},{320,384},{384,448},... | collective-permute-start | bytes 49160 | tf_op jit(solution)/shard_map/ppermute | solution.py:12
Sparse Core Ops, SparseCore 0:
  157.9 830.6 all-reduce.2
